TPU v7x, 32 devices: a whole 2x2x4 slice. The times are simulated.
32 devices in a mesh: shards: 4 (over x, core), context: 2 (over y), tensor: 4 (over z).
Axes of the slice: x: 2, y: 2, z: 4, core: 2. Of those that a mesh axis runs over, the one named last changes fastest.
Arguments:
- tokens: bfloat16 [8192, 1280], P(('shards', 'context')), may hold values from -6 to 6
- cotangent: bfloat16 [8192, 1280], P(('shards', 'context')), may hold values from -6 to 6
- segments: int32 [8192], P(('shards', 'context')), may hold values from 0 to 1024, as said below
- positions: int32 [8192], P(('shards', 'context')), may hold values from 0 to 1279, as said below
- w_query: bfloat16 [1280, 1280], P('shards', 'tensor'), may hold values from -0.15625 to 0.15625
- w_key: bfloat16 [1280, 1280], P('shards', 'tensor'), may hold values from -0.15625 to 0.15625
- w_value: bfloat16 [1280, 1280], P('shards', 'tensor'), may hold values from -0.15625 to 0.15625
- w_output: bfloat16 [1280, 1280], P('tensor', 'shards'), may hold values from -0.15625 to 0.15625
- w_up: bfloat16 [1280, 5120], P('shards', 'tensor'), may hold values from -0.15625 to 0.15625
- w_gate: bfloat16 [1280, 5120], P('shards', 'tensor'), may hold values from -0.15625 to 0.15625
- w_down: bfloat16 [5120, 1280], P('tensor', 'shards'), may hold values from -0.078125 to 0.078125
- scale_qk: float32 [1280], P('tensor'), may hold values from 1 to 1.6
- alpha_attn: float32 [1280], replicated, may hold values from 0.15 to 0.6
- alpha_mlp: float32 [1280], replicated, may hold values from 0.15 to 0.6
- scale_up: float32 [5120], P('tensor'), may hold values from 0.25 to 1.75
- scale_gate: float32 [5120], P('tensor'), may hold values from 0.25 to 1.75
Outputs:
- block_out: bfloat16 [8192, 1280], P(('shards', 'context'))
- grad_tokens: bfloat16 [8192, 1280], P(('shards', 'context'))
- grad_query: float32 [1280, 1280], P('shards', 'tensor')
- grad_key: float32 [1280, 1280], P('shards', 'tensor')
- grad_value: float32 [1280, 1280], P('shards', 'tensor')
- grad_output: float32 [1280, 1280], P('tensor', 'shards')
- grad_up: float32 [1280, 5120], P('shards', 'tensor')
- grad_gate: float32 [1280, 5120], P('shards', 'tensor')
- grad_down: float32 [5120, 1280], P('tensor', 'shards')
- grad_scale_qk: float32 [1280], P('tensor')
- grad_alpha_attn: float32 [1280], replicated
- grad_alpha_mlp: float32 [1280], replicated
- grad_scale_up: float32 [5120], P('tensor')
- grad_scale_gate: float32 [5120], P('tensor')
Inputs may be any that keep to these rules, and one draw needn't show every extreme that they name: `segments`: each run of 1024 tokens in order (one device of shards and context) holds first 512 prompt tokens (id 0), the prompt's tokens lying in order over the group, then 512 slots filled with whole continuations of 1 to 256 tokens each, one of exactly 256; a continuation's tokens are consecutive and its id is shared by no other continuation of the group. `positions`: A prompt token's position is its index in the group's prompt; a continuation token's is 1024 plus its offset in its continuation.
All inputs are finite; a program needn't handle non-finite values.
Results may differ from a plain program's by a relative error of at most 0.02.
Values may be sent and summed in bfloat16 or wider, within the bound.
No kernel may reach another device: no remote copies, remote signals or barrier semaphores. Data moves between devices by JAX's collectives and lax.ppermute only.
A program may use at most 192 MiB of HBM per device.

v0:
```python
import math
import jax
import jax.numpy as jnp
from jax import lax
from jax.sharding import PartitionSpec as P

HD = 64
CONT_DEV = 2
CONT_LEN = 256
EPSILON = 1e-06
MASKED = -1e30


def renorm(vector):
    return vector * lax.rsqrt(jnp.mean(vector * vector, axis=-1, keepdims=True) + EPSILON)


def rotate(values, cosine_table, sine_table):
    half_size = values.shape[-1] // 2
    first_half = values[..., :half_size]
    second_half = values[..., half_size:]
    return jnp.concatenate(
        [
            first_half * cosine_table - second_half * sine_table,
            second_half * cosine_table + first_half * sine_table,
        ],
        axis=-1,
    )


def head_norm(raw_heads, cosine_table, sine_table, factor):
    turned = rotate(raw_heads, cosine_table[:, None, :], sine_table[:, None, :])
    return factor * turned * lax.rsqrt(jnp.sum(turned * turned, axis=-1, keepdims=True) + EPSILON)


def residual_step(hidden, branch, alpha):
    return renorm(hidden + alpha * (renorm(branch) - hidden))


def swiglu(up_proj, gate_proj, scale_up, scale_gate):
    return scale_up * up_proj * jax.nn.silu(scale_gate * gate_proj)


def phase_tables(positions, head_size):
    half_size = head_size // 2
    frequency = 10000.0 ** (-(jnp.arange(half_size, dtype=jnp.float32) * 2.0 / head_size))
    phases = positions.astype(jnp.float32)[:, None] * frequency[None, :]
    return (jnp.cos(phases), jnp.sin(phases))


def outer_sum(left, right):
    return lax.dot_general(
        left, right, (((0,), (0,)), ((), ())), preferred_element_type=jnp.float32
    )


def back_product(gradient, weight):
    return lax.dot_general(
        gradient, weight, (((1,), (1,)), ((), ())), preferred_element_type=jnp.float32
    )


def to_heads(flat, head_size):
    return jnp.swapaxes(flat.reshape(flat.shape[0], -1, head_size), 0, 1)


def from_heads(stacked):
    return jnp.swapaxes(stacked, 0, 1).reshape(stacked.shape[1], -1)


def on_device(
    tokens,
    cotangent,
    segments,
    positions,
    w_query,
    w_key,
    w_value,
    w_output,
    w_up,
    w_gate,
    w_down,
    scale_qk,
    alpha_attn,
    alpha_mlp,
    scale_up,
    scale_gate,
):
    full_query, full_key, full_value, full_output, full_up, full_gate, full_down = (
        lax.all_gather(w_query, "shards", axis=0, tiled=True),
        lax.all_gather(w_key, "shards", axis=0, tiled=True),
        lax.all_gather(w_value, "shards", axis=0, tiled=True),
        lax.all_gather(w_output, "shards", axis=1, tiled=True),
        lax.all_gather(w_up, "shards", axis=0, tiled=True),
        lax.all_gather(w_gate, "shards", axis=0, tiled=True),
        lax.all_gather(w_down, "shards", axis=1, tiled=True),
    )
    row_count = tokens.shape[0]
    prompt_rows = row_count - CONT_DEV * CONT_LEN
    heads_local = scale_qk.shape[0] // HD
    multiplier = math.sqrt(HD)
    factor = scale_qk.reshape(heads_local, HD)
    cosine_table, sine_table = phase_tables(positions, HD)

    def normalize(raw_heads, factor_heads):
        return head_norm(raw_heads, cosine_table, sine_table, factor_heads)

    query_raw = jnp.dot(tokens, full_query, preferred_element_type=jnp.float32).reshape(
        row_count, heads_local, HD
    )
    key_raw = jnp.dot(tokens, full_key, preferred_element_type=jnp.float32).reshape(
        row_count, heads_local, HD
    )
    value_low = jnp.dot(tokens, full_value, preferred_element_type=jnp.float32).astype(jnp.bfloat16)
    query_normed, query_back = jax.vjp(normalize, query_raw, factor)
    key_normed, key_back = jax.vjp(normalize, key_raw, factor)
    query_low = query_normed.astype(jnp.bfloat16).reshape(row_count, -1)
    key_low = key_normed.astype(jnp.bfloat16).reshape(row_count, -1)
    prompt_keys, prompt_values = (
        lax.all_gather(key_low[:prompt_rows], "context", axis=0, tiled=True),
        lax.all_gather(value_low[:prompt_rows], "context", axis=0, tiled=True),
    )
    prompt_total = prompt_keys.shape[0]
    key_positions = jnp.concatenate(
        [jnp.arange(prompt_total, dtype=jnp.int32), positions[prompt_rows:]]
    )
    key_segments = jnp.concatenate([jnp.zeros((prompt_total,), jnp.int32), segments[prompt_rows:]])
    allowed = (key_positions[None, :] <= positions[:, None]) & (
        (key_segments[None, :] == 0) | (key_segments[None, :] == segments[:, None])
    )
    key_heads = to_heads(jnp.concatenate([prompt_keys, key_low[prompt_rows:]], axis=0), HD)
    value_heads = to_heads(jnp.concatenate([prompt_values, value_low[prompt_rows:]], axis=0), HD)
    key_heads, value_heads = (key_heads, value_heads)
    query_heads = to_heads(query_low, HD)

    def masked_scores(query_head, key_head):
        scores = multiplier * jnp.einsum(
            "qd,kd->qk", query_head, key_head, preferred_element_type=jnp.float32
        )
        return jnp.where(allowed, scores, MASKED)

    def attend_head(operands):
        query_head, key_head, value_head = operands
        scores = masked_scores(query_head, key_head)
        row_peak = jnp.max(scores, axis=1, keepdims=True)
        weights = jnp.exp(scores - row_peak)
        row_total = jnp.sum(weights, axis=1, keepdims=True)
        softmax_low = (weights / row_total).astype(jnp.bfloat16)
        head_out = jnp.dot(softmax_low, value_head, preferred_element_type=jnp.float32).astype(
            jnp.bfloat16
        )
        return (head_out, (row_peak + jnp.log(row_total))[:, 0])

    mixed_heads, log_totals = lax.map(attend_head, (query_heads, key_heads, value_heads))
    mixed_low = from_heads(mixed_heads)
    attn_terms = jnp.dot(mixed_low, full_output, preferred_element_type=jnp.float32)
    attn_out = lax.psum(attn_terms, "tensor")
    after_attn, attn_back = jax.vjp(residual_step, tokens.astype(jnp.float32), attn_out, alpha_attn)
    after_low = after_attn.astype(jnp.bfloat16)
    up_proj = jnp.dot(after_low, full_up, preferred_element_type=jnp.float32)
    gate_proj = jnp.dot(after_low, full_gate, preferred_element_type=jnp.float32)
    inner, swiglu_back = jax.vjp(swiglu, up_proj, gate_proj, scale_up, scale_gate)
    inner_low = inner.astype(jnp.bfloat16)
    merged_terms = jnp.dot(inner_low, full_down, preferred_element_type=jnp.float32)
    merged = lax.psum(merged_terms, "tensor")
    block_whole, out_back = jax.vjp(residual_step, after_attn, merged, alpha_mlp)
    block_low = block_whole.astype(jnp.bfloat16)
    grad_after, grad_merged, grad_alpha_mlp = out_back(cotangent.astype(jnp.float32))
    merged_grad_low = grad_merged.astype(jnp.bfloat16)
    grad_down = outer_sum(inner_low, merged_grad_low)
    grad_up_proj, grad_gate_proj, grad_scale_up, grad_scale_gate = swiglu_back(
        back_product(merged_grad_low, full_down)
    )
    up_grad_low = grad_up_proj.astype(jnp.bfloat16)
    gate_grad_low = grad_gate_proj.astype(jnp.bfloat16)
    grad_up = outer_sum(after_low, up_grad_low)
    grad_gate = outer_sum(after_low, gate_grad_low)
    input_terms = back_product(up_grad_low, full_up) + back_product(gate_grad_low, full_gate)
    grad_after = grad_after + lax.psum(input_terms, "tensor")
    grad_tokens_direct, grad_attn, grad_alpha_attn = attn_back(grad_after)
    attn_grad_low = grad_attn.astype(jnp.bfloat16)
    grad_output = outer_sum(mixed_low, attn_grad_low)
    grad_mixed_heads = to_heads(back_product(attn_grad_low, full_output).astype(jnp.bfloat16), HD)
    back_keys, back_values = (key_heads, value_heads)

    def head_backward(operands):
        query_head, key_head, value_head, grad_head, log_total = operands
        softmax_full = jnp.exp(masked_scores(query_head, key_head) - log_total[:, None])
        grad_softmax = jnp.einsum(
            "qd,kd->qk", grad_head, value_head, preferred_element_type=jnp.float32
        )
        weighted = jnp.sum(softmax_full * grad_softmax, axis=1, keepdims=True)
        grad_scores = (softmax_full * (grad_softmax - weighted)).astype(jnp.bfloat16)
        grad_query_head = multiplier * jnp.dot(
            grad_scores, key_head, preferred_element_type=jnp.float32
        )
        grad_key_head = multiplier * outer_sum(grad_scores, query_head)
        grad_value_head = outer_sum(softmax_full.astype(jnp.bfloat16), grad_head)
        return (grad_query_head, grad_key_head, grad_value_head)

    grad_query_heads, grad_key_heads, grad_value_heads = lax.map(
        head_backward, (query_heads, back_keys, back_values, grad_mixed_heads, log_totals)
    )
    grad_key_flat = from_heads(grad_key_heads)
    grad_value_flat = from_heads(grad_value_heads)
    prompt_grad_keys, prompt_grad_values = (
        lax.psum_scatter(
            grad_key_flat[:prompt_total].astype(jnp.bfloat16),
            "context",
            scatter_dimension=0,
            tiled=True,
        ).astype(jnp.float32),
        lax.psum_scatter(
            grad_value_flat[:prompt_total].astype(jnp.bfloat16),
            "context",
            scatter_dimension=0,
            tiled=True,
        ).astype(jnp.float32),
    )
    grad_key_rows = jnp.concatenate([prompt_grad_keys, grad_key_flat[prompt_total:]], axis=0)
    grad_value_rows = jnp.concatenate([prompt_grad_values, grad_value_flat[prompt_total:]], axis=0)
    grad_query_raw, grad_factor_query = query_back(
        from_heads(grad_query_heads).reshape(row_count, heads_local, HD)
    )
    grad_key_raw, grad_factor_key = key_back(grad_key_rows.reshape(row_count, heads_local, HD))
    query_grad_low = grad_query_raw.reshape(row_count, -1).astype(jnp.bfloat16)
    key_grad_low = grad_key_raw.reshape(row_count, -1).astype(jnp.bfloat16)
    value_grad_low = grad_value_rows.astype(jnp.bfloat16)
    grad_query = outer_sum(tokens, query_grad_low)
    grad_key = outer_sum(tokens, key_grad_low)
    grad_value = outer_sum(tokens, value_grad_low)
    token_terms = (
        back_product(query_grad_low, full_query)
        + back_product(key_grad_low, full_key)
        + back_product(value_grad_low, full_value)
    )
    grad_tokens = (
        grad_tokens_direct
        + lax.psum(token_terms.astype(jnp.bfloat16), "tensor").astype(jnp.float32)
    ).astype(jnp.bfloat16)
    grad_scale_qk = (grad_factor_query + grad_factor_key).reshape(-1)
    shard_query, shard_key, shard_value, shard_output, shard_up, shard_gate, shard_down = (
        lax.psum_scatter(
            grad_query.astype(jnp.bfloat16), "shards", scatter_dimension=0, tiled=True
        ).astype(jnp.float32),
        lax.psum_scatter(
            grad_key.astype(jnp.bfloat16), "shards", scatter_dimension=0, tiled=True
        ).astype(jnp.float32),
        lax.psum_scatter(
            grad_value.astype(jnp.bfloat16), "shards", scatter_dimension=0, tiled=True
        ).astype(jnp.float32),
        lax.psum_scatter(
            grad_output.astype(jnp.bfloat16), "shards", scatter_dimension=1, tiled=True
        ).astype(jnp.float32),
        lax.psum_scatter(
            grad_up.astype(jnp.bfloat16), "shards", scatter_dimension=0, tiled=True
        ).astype(jnp.float32),
        lax.psum_scatter(
            grad_gate.astype(jnp.bfloat16), "shards", scatter_dimension=0, tiled=True
        ).astype(jnp.float32),
        lax.psum_scatter(
            grad_down.astype(jnp.bfloat16), "shards", scatter_dimension=1, tiled=True
        ).astype(jnp.float32),
    )
    part_query, part_key, part_value, part_output, part_up, part_gate, part_down = (
        lax.psum_scatter(
            shard_query.astype(jnp.bfloat16), "context", scatter_dimension=0, tiled=True
        ).astype(jnp.float32),
        lax.psum_scatter(
            shard_key.astype(jnp.bfloat16), "context", scatter_dimension=0, tiled=True
        ).astype(jnp.float32),
        lax.psum_scatter(
            shard_value.astype(jnp.bfloat16), "context", scatter_dimension=0, tiled=True
        ).astype(jnp.float32),
        lax.psum_scatter(
            shard_output.astype(jnp.bfloat16), "context", scatter_dimension=1, tiled=True
        ).astype(jnp.float32),
        lax.psum_scatter(
            shard_up.astype(jnp.bfloat16), "context", scatter_dimension=0, tiled=True
        ).astype(jnp.float32),
        lax.psum_scatter(
            shard_gate.astype(jnp.bfloat16), "context", scatter_dimension=0, tiled=True
        ).astype(jnp.float32),
        lax.psum_scatter(
            shard_down.astype(jnp.bfloat16), "context", scatter_dimension=1, tiled=True
        ).astype(jnp.float32),
    )
    sum_query, sum_key, sum_value, sum_output, sum_up, sum_gate, sum_down = (
        lax.all_gather(part_query.astype(jnp.bfloat16), "context", axis=0, tiled=True).astype(
            part_query.dtype
        ),
        lax.all_gather(part_key.astype(jnp.bfloat16), "context", axis=0, tiled=True).astype(
            part_key.dtype
        ),
        lax.all_gather(part_value.astype(jnp.bfloat16), "context", axis=0, tiled=True).astype(
            part_value.dtype
        ),
        lax.all_gather(part_output.astype(jnp.bfloat16), "context", axis=1, tiled=True).astype(
            part_output.dtype
        ),
        lax.all_gather(part_up.astype(jnp.bfloat16), "context", axis=0, tiled=True).astype(
            part_up.dtype
        ),
        lax.all_gather(part_gate.astype(jnp.bfloat16), "context", axis=0, tiled=True).astype(
            part_gate.dtype
        ),
        lax.all_gather(part_down.astype(jnp.bfloat16), "context", axis=1, tiled=True).astype(
            part_down.dtype
        ),
    )
    total_scale_qk, total_alpha_attn, total_alpha_mlp, total_scale_up, total_scale_gate = lax.psum(
        (grad_scale_qk, grad_alpha_attn, grad_alpha_mlp, grad_scale_up, grad_scale_gate),
        ("shards", "context"),
    )
    return (
        block_low,
        grad_tokens,
        sum_query,
        sum_key,
        sum_value,
        sum_output,
        sum_up,
        sum_gate,
        sum_down,
        total_scale_qk,
        total_alpha_attn,
        total_alpha_mlp,
        total_scale_up,
        total_scale_gate,
    )


def solution(mesh):
    in_specs = (
        P(("shards", "context"), None),
        P(("shards", "context"), None),
        P(("shards", "context")),
        P(("shards", "context")),
        P("shards", "tensor"),
        P("shards", "tensor"),
        P("shards", "tensor"),
        P("tensor", "shards"),
        P("shards", "tensor"),
        P("shards", "tensor"),
        P("tensor", "shards"),
        P("tensor"),
        P(),
        P(),
        P("tensor"),
        P("tensor"),
    )
    out_specs = (
        P(("shards", "context"), None),
        P(("shards", "context"), None),
        P("shards", "tensor"),
        P("shards", "tensor"),
        P("shards", "tensor"),
        P("tensor", "shards"),
        P("shards", "tensor"),
        P("shards", "tensor"),
        P("tensor", "shards"),
        P("tensor"),
        P(),
        P(),
        P("tensor"),
        P("tensor"),
    )
    return jax.shard_map(
        on_device, mesh=mesh, in_specs=in_specs, out_specs=out_specs, check_vma=False
    )
```

profile of v0, /device:TPU:0, one launch (start us, length us, event | category | flops | bytes accessed | tf_op | source)
XLA Modules:
  0.0 1299.2 jit_solution(2730937836505166477)
XLA Ops:
  11.3 11.3 all_gather.48
  22.7 10.1 all_gather.49
  32.8 3.2 fusion.70
  39.9 10.6 all_gather.50
  55.8 9.5 all_gather.51
  66.5 10.8 all_gather.52
  81.5 57.1 %while.28 = (s32[]{:T(128)}, bf16[5,1024,64]{1,2,0:T(8,128)(2,1)S(1)}, f32[5,1024]{1,0:T(8,128)S(1)}, bf16[5,1024,64]{2,1,0:T(8,128)(2,1)}, bf16[5,1536,64]{2,1,...) while((s32[]{:T(128)}, ...), condition=%wide.region_5.6_spmd.clone, body=%wide.region_2.5_spmd.clone.sunk | while | flops 421592064 | bytes 45289628 | solution.py:154
  81.6 3.4 fusion.135
  88.8 4.2 fusion.137
  93.0 3.4 fusion.135
  100.2 4.2 fusion.137
  104.4 3.4 fusion.135
  111.6 4.2 fusion.137
  115.8 3.4 fusion.135
  123.0 4.2 fusion.137
  127.2 3.4 fusion.135
  134.4 4.2 fusion.137
  140.0 9.3 all_gather.53
  150.3 3.9 fusion.72
  156.1 188.1 %all-reduce.11.cloned.1.call-done = f32[1024,1280]{1,0:T(8,128)} async-done(((f32[1024,1280]{1,0:T(8,128)}), f32[1024,1280]{1,0:T(8,128)}) %all-reduce.11.cloned.1.call-update) | async-done | bytes 5242896 | tf_op jit(solution)/shard_map/psum | solution.py:157
  352.4 8.1 fusion.73
  360.6 8.7 multiply_convert_fusion.4
  369.3 8.7 fusion.74
  378.4 187.5 %all-reduce.13.cloned.1.call-done = f32[1024,1280]{1,0:T(8,128)} async-done(((f32[1024,1280]{1,0:T(8,128)}), f32[1024,1280]{1,0:T(8,128)}) %all-reduce.13.cloned.1.call-update) | async-done | bytes 5242896 | tf_op jit(solution)/shard_map/psum | solution.py:165
  570.0 4.7 fusion.49
  574.8 3.1 multiply_reduce_fusion.7
  581.1 9.5 multiply_reduce_fusion.1
  590.7 3.6 fusion.75
  595.0 5.5 convolution_add_fusion
  600.8 187.8 %all-reduce.15.cloned.1.call-done = f32[1024,1280]{1,0:T(8,128)} async-done(((f32[1024,1280]{1,0:T(8,128)}), f32[1024,1280]{1,0:T(8,128)}) %all-reduce.15.cloned.1.call-update) | async-done | bytes 5242896 | tf_op jit(solution)/shard_map/psum | solution.py:179
  788.5 9.5 multiply_reduce_fusion.3
  798.1 11.6 multiply_reduce_fusion.4
  814.4 68.5 %while.29 = (s32[]{:T(128)}, f32[5,1024,64]{1,2,0:T(8,128)}, f32[5,1536,64]{1,2,0:T(8,128)}, bf16[5,1536,64]{1,2,0:T(8,128)(2,1)}, bf16[5,1024,64]{2,1,0:T(8,128...) while((s32[]{:T(128)}, f32[5,1024,64]{1,2,0:T(8,128)}, ...), condition=%wide.region_19.20_spmd.clone, body=%wide.region_17.19_spmd.clone.sunk | while | flops 1027243008 | bytes 50515088 | solution.py:201
  816.5 4.5 multiply_reduce_fusion.18
  830.2 4.5 multiply_reduce_fusion.18
  843.9 4.5 multiply_reduce_fusion.18
  857.5 4.5 multiply_reduce_fusion.18
  871.3 4.5 multiply_reduce_fusion.18
  887.7 3.8 convolution_convert_fusion.3
  893.8 6.8 convolution_convert_fusion
  902.3 6.7 convolution_convert_fusion.2
  909.2 7.5 convolution_convert_fusion.1
  921.6 4.0 fusion.57
  945.7 40.9 %reduce-scatter.45.cloned.1.call-done = bf16[1280,320]{0,1:T(8,128)(2,1)} async-done(((bf16[1280,1280]{0,1:T(8,128)(2,1)}), bf16[1280,320]{0,1:T(8,128)(2,1)}) %reduce-scatter.45.cloned.1.call-update) | async-done | bytes 819216 | tf_op jit(solution)/shard_map/reduce_scatter | solution.py:261
  986.7 40.9 %reduce-scatter.37.cloned.1.call-done = bf16[320,1280]{1,0:T(8,128)(2,1)} async-done(((bf16[1280,1280]{1,0:T(8,128)(2,1)}), bf16[320,1280]{1,0:T(8,128)(2,1)}) %reduce-scatter.37.cloned.1.call-update) | async-done | bytes 819216 | tf_op jit(solution)/shard_map/reduce_scatter | solution.py:255
  1027.8 40.9 %reduce-scatter.41.cloned.1.call-done = bf16[320,1280]{1,0:T(8,128)(2,1)} async-done(((bf16[1280,1280]{1,0:T(8,128)(2,1)}), bf16[320,1280]{1,0:T(8,128)(2,1)}) %reduce-scatter.41.cloned.1.call-update) | async-done | bytes 819216 | tf_op jit(solution)/shard_map/reduce_scatter | solution.py:258
  1068.8 27.5 %reduce-scatter.57.cloned.1.call-done = bf16[320,320]{1,0:T(8,128)(2,1)} async-done(((bf16[1280,320]{1,0:T(8,128)(2,1)}), bf16[320,320]{1,0:T(8,128)(2,1)}) %reduce-scatter.57.cloned.1.call-update) | async-done | bytes 204816
  1096.3 27.3 %reduce-scatter.53.cloned.1.call-done = bf16[320,320]{1,0:T(8,128)(2,1)} async-done(((bf16[1280,320]{1,0:T(8,128)(2,1)}), bf16[320,320]{1,0:T(8,128)(2,1)}) %reduce-scatter.53.cloned.1.call-update) | async-done | bytes 204816
  1123.7 3.9 fusion.77
  1127.7 3.8 fusion.76
  1131.5 19.6 %reduce-scatter.49.cloned.1.call-done = bf16[320,320]{1,0:T(8,128)(2,1)} async-done(((bf16[1280,320]{1,0:T(8,128)(2,1)}), bf16[320,320]{1,0:T(8,128)(2,1)}) %reduce-scatter.49.cloned.1.call-update) | async-done | bytes 204816
  1151.3 7.1 add_convert_fusion.1
  1158.5 26.4 %all-reduce.5 = (f32[320]{0:T(512)}, f32[1280]{0:T(1024)}, f32[1280]{0:T(1024)}, f32[1280]{0:T(1024)}, f32[1280]{0:T(1024)}) all-reduce(f32[320]{0:T(512)S(1)} %add.196, f32[1280]{0:T(1024)S(1)} %copy-done.58, f32[1280]{0:T(1024)S(1)} %copy-done.57, ...), channel_id=1, replica_groups=mesh['shards'=4,'context'=2,'tensor'=4] {'shards','context'}, use_global_device_ids=true, to_apply=%region_41.42 | all-reduce | flops 5440 | bytes 43520 | tf_op jit(solution)/shard_map/psum | solution.py:311
  1184.9 5.7 all_gather.60
  1191.6 19.3 %all_gather.63 = bf16[1280,320]{0,1:T(8,128)(2,1)S(1)} all-gather(bf16[1280,160]{0,1:T(8,128)(2,1)} %reduce-scatter.47.cloned.1.call-done), channel_id=1, replica_groups=mesh['shards'=4,'context'=2,'tensor'=4] {'context'}, dimensions={1}, use_global_device_ids=true | all-gather | bytes 1228800 | tf_op jit(solution)/shard_map/all_gather | solution.py:307
  1212.5 13.6 %all_gather.61 = bf16[320,1280]{1,0:T(8,128)(2,1)S(1)} all-gather(bf16[160,1280]{1,0:T(8,128)(2,1)} %reduce-scatter.39.cloned.1.call-done), channel_id=1, replica_groups=mesh['shards'=4,'context'=2,'tensor'=4] {'context'}, dimensions={0}, use_global_device_ids=true | all-gather | bytes 1228800 | tf_op jit(solution)/shard_map/all_gather | solution.py:301
  1227.3 7.2 reduce-scatter.43.cloned.1.call-done
  1234.5 13.6 %all_gather.62 = bf16[320,1280]{1,0:T(8,128)(2,1)S(1)} all-gather(bf16[160,1280]{1,0:T(8,128)(2,1)} %reduce-scatter.43.cloned.1.call-done), channel_id=1, replica_groups=mesh['shards'=4,'context'=2,'tensor'=4] {'context'}, dimensions={0}, use_global_device_ids=true | all-gather | bytes 1228800 | tf_op jit(solution)/shard_map/all_gather | solution.py:304
  1250.1 5.9 all_gather.59
  1256.9 8.7 reduce-scatter.55.cloned.1.call-done
  1265.5 5.7 all_gather.58
  1272.1 7.1 reduce-scatter.51.cloned.1.call-done
  1279.1 5.7 all_gather.57
  1285.7 5.7 add_convert_fusion
  (343 shorter events, 150.5 us)
Async XLA Ops:
  8.0 336.2 %all-reduce.11.cloned.1.call-start = ((), (), s32[]{:S(2)}) async-start(), calls=%async_computation.16 | async-start | bytes 10485760 | tf_op jit(solution)/shard_map/psum | solution.py:157
  22.7 13.3 %copy-start.24 = (bf16[1280,320]{1,0:T(8,128)(2,1)}, bf16[1280,320]{1,0:T(8,128)(2,1)S(1)}, u32[]{:S(2)}) copy-start(bf16[1280,320]{1,0:T(8,128)(2,1)S(1)} %all_gather.48) | copy-start | bytes 2457604
  22.7 13.3 %copy-start.15 = (bf16[1024,1280]{1,0:T(8,128)(2,1)S(1)}, bf16[1024,1280]{1,0:T(8,128)(2,1)}, u32[]{:S(2)}) copy-start(bf16[1024,1280]{1,0:T(8,128)(2,1)} %param.20) | copy-start | bytes 7864324
  38.5 13.1 %copy-start.43 = (f32[1024,5]{0,1:T(8,128)}, f32[1024,5]{0,1:T(8,128)S(1)}, u32[]{:S(2)}) copy-start(f32[1024,5]{0,1:T(8,128)S(1)} %add_rsqrt_fusion) | copy-start | bytes 61444
  39.4 12.1 copy-start.45
  39.5 12.1 copy-start.55
  51.6 13.7 %copy-start.16 = (bf16[1024,1280]{1,0:T(8,128)(2,1)S(1)}, bf16[1024,1280]{1,0:T(8,128)(2,1)}, u32[]{:S(2)}) copy-start(bf16[1024,1280]{1,0:T(8,128)(2,1)} %param.20) | copy-start | bytes 7864324
  66.4 15.1 %copy-start.35 = (bf16[5,1024,64]{1,2,0:T(8,128)(2,1)S(1)}, bf16[5,1024,64]{1,2,0:T(8,128)(2,1)}, u32[]{:S(2)}) copy-start(bf16[5,1024,64]{1,2,0:T(8,128)(2,1)} %custom-call) | copy-start | bytes 1966084
  66.4 15.1 %copy-start.59 = (s32[1024]{0:T(1024)S(1)}, s32[1024]{0:T(1024)}, u32[]{:S(2)}) copy-start(s32[1024]{0:T(1024)} %param.23) | copy-start | bytes 12292
  66.5 15.1 %copy-start.64 = (s32[1024]{0:T(1024)S(1)}, s32[1024]{0:T(1024)}, u32[]{:S(2)}) copy-start(s32[1024]{0:T(1024)} %param.22) | copy-start | bytes 12292
  138.6 15.6 %copy-start.36 = (bf16[5,1024,64]{1,2,0:T(8,128)(2,1)}, bf16[5,1024,64]{1,2,0:T(8,128)(2,1)S(1)}, u32[]{:S(2)}) copy-start(bf16[5,1024,64]{1,2,0:T(8,128)(2,1)S(1)} %get-tuple-element.106) | copy-start | bytes 1966084
  154.3 198.1 %all-gather.6.cloned.1.call-start = ((), (), s32[]{:S(2)}) async-start(), calls=%async_computation.18 | async-start | bytes 4096000 | tf_op jit(solution)/shard_map/all_gather | solution.py:95
  154.9 192.4 %copy-start.53 = (f32[1280]{0:T(1024)S(1)}, f32[1280]{0:T(1024)}, u32[]{:S(2)}) copy-start(f32[1280]{0:T(1024)} %param.32) | copy-start | bytes 15364
  154.9 205.7 %all-gather.4.cloned.1.call-start = ((), (), s32[]{:S(2)}) async-start(), calls=%async_computation.17 | async-start | bytes 4096000 | tf_op jit(solution)/shard_map/all_gather | solution.py:94
  155.5 213.8 %all-gather.8.cloned.1.call-start = ((), (), s32[]{:S(2)}) async-start(), calls=%async_computation.19 | async-start | bytes 4096000 | tf_op jit(solution)/shard_map/all_gather | solution.py:96
  156.0 410.0 %all-reduce.13.cloned.1.call-start = ((), (), s32[]{:S(2)}) async-start(), calls=%async_computation.20 | async-start | bytes 10485760 | tf_op jit(solution)/shard_map/psum | solution.py:165
  352.3 8.2 copy-start.30
  352.4 8.2 copy-start.69
  352.4 8.2 copy-start.70
  378.0 191.1 %copy-start.4 = (bf16[1024,1280]{1,0:T(8,128)(2,1)S(1)}, bf16[1024,1280]{1,0:T(8,128)(2,1)}, u32[]{:S(2)}) copy-start(bf16[1024,1280]{1,0:T(8,128)(2,1)} %param.21) | copy-start | bytes 7864324
  378.0 191.1 %copy-start.52 = (f32[1280]{0:T(1024)S(1)}, f32[1280]{0:T(1024)}, u32[]{:S(2)}) copy-start(f32[1280]{0:T(1024)} %param.33) | copy-start | bytes 15364
  378.0 410.5 %all-reduce.15.cloned.1.call-start = ((), (), s32[]{:S(2)}) async-start(), calls=%async_computation.21 | async-start | bytes 10485760 | tf_op jit(solution)/shard_map/psum | solution.py:179
  569.0 5.7 slice-start
  570.0 4.8 slice-start.1
  574.8 6.3 slice-start.4
  581.0 9.6 copy-start.32
  581.1 9.6 copy-start.67
  600.5 319.1 %reduce-scatter.33.cloned.1.call-start = ((), (), s32[]{:S(2)}) async-start(), calls=%async_computation.22 | async-start | bytes 983040 | tf_op jit(solution)/shard_map/reduce_scatter | solution.py:207
  788.5 9.5 copy-start.6
  798.0 11.7 slice-start.2
  798.0 11.7 slice-start.3
  885.3 36.2 %reduce-scatter.35.cloned.1.call-start = ((), (), s32[]{:S(2)}) async-start(), calls=%async_computation.23 | async-start | bytes 983040 | tf_op jit(solution)/shard_map/reduce_scatter | solution.py:213
  887.4 6.4 copy-start.33
  887.4 58.2 %reduce-scatter.61.cloned.1.call-start = ((), (), s32[]{:S(2)}) async-start(), calls=%async_computation.37 | async-start | bytes 1228800
  893.7 93.0 %reduce-scatter.45.cloned.1.call-start = ((), (), s32[]{:S(2)}) async-start(), calls=%async_computation.29 | async-start | bytes 4096000 | tf_op jit(solution)/shard_map/reduce_scatter | solution.py:261
  900.6 127.1 %reduce-scatter.37.cloned.1.call-start = ((), (), s32[]{:S(2)}) async-start(), calls=%async_computation.25 | async-start | bytes 4096000 | tf_op jit(solution)/shard_map/reduce_scatter | solution.py:255
  909.1 159.6 %reduce-scatter.41.cloned.1.call-start = ((), (), s32[]{:S(2)}) async-start(), calls=%async_computation.27 | async-start | bytes 4096000 | tf_op jit(solution)/shard_map/reduce_scatter | solution.py:258
  916.7 179.5 %reduce-scatter.57.cloned.1.call-start = ((), (), s32[]{:S(2)}) async-start(), calls=%async_computation.35 | async-start | bytes 1228800
  921.5 6.4 copy-start.8
  921.5 6.4 copy-start.10
  921.5 6.4 copy-start.12
  921.5 6.4 copy-start.14
  921.6 6.4 copy-start.44
  921.6 6.4 copy-start.46
  921.6 6.4 copy-start.56
  927.8 195.8 %reduce-scatter.53.cloned.1.call-start = ((), (), s32[]{:S(2)}) async-start(), calls=%async_computation.33 | async-start | bytes 1228800
  937.8 213.3 %reduce-scatter.49.cloned.1.call-start = ((), (), s32[]{:S(2)}) async-start(), calls=%async_computation.31 | async-start | bytes 1228800
  942.3 181.5 %copy-start.27 = (bf16[1280,320]{1,0:T(8,128)(2,1)S(1)}, bf16[1280,320]{1,0:T(8,128)(2,1)}, u32[]{:S(2)}) copy-start(bf16[1280,320]{1,0:T(8,128)(2,1)} %copy-done.26) | copy-start | bytes 2457604
  944.6 240.3 %reduce-scatter.63.cloned.1.call-start = ((), (), s32[]{:S(2)}) async-start(), calls=%async_computation.38 | async-start | bytes 368640
  945.7 245.9 %reduce-scatter.47.cloned.1.call-start = ((), (), s32[]{:S(2)}) async-start(), calls=%async_computation.30 | async-start | bytes 1228800 | tf_op jit(solution)/shard_map/reduce_scatter | solution.py:284
  986.7 225.8 %reduce-scatter.39.cloned.1.call-start = ((), (), s32[]{:S(2)}) async-start(), calls=%async_computation.26 | async-start | bytes 1228800 | tf_op jit(solution)/shard_map/reduce_scatter | solution.py:278
  1027.7 206.8 %reduce-scatter.43.cloned.1.call-start = ((), (), s32[]{:S(2)}) async-start(), calls=%async_computation.28 | async-start | bytes 1228800 | tf_op jit(solution)/shard_map/reduce_scatter | solution.py:281
  1068.7 181.4 %reduce-scatter.59.cloned.1.call-start = ((), (), s32[]{:S(2)}) async-start(), calls=%async_computation.36 | async-start | bytes 368640 | tf_op jit(solution)/shard_map/reduce_scatter | solution.py:272
  1096.3 169.3 %reduce-scatter.55.cloned.1.call-start = ((), (), s32[]{:S(2)}) async-start(), calls=%async_computation.34 | async-start | bytes 368640 | tf_op jit(solution)/shard_map/reduce_scatter | solution.py:269
  1123.7 155.5 %reduce-scatter.51.cloned.1.call-start = ((), (), s32[]{:S(2)}) async-start(), calls=%async_computation.32 | async-start | bytes 368640 | tf_op jit(solution)/shard_map/reduce_scatter | solution.py:266
  1127.7 23.6 %copy-start.23 = (bf16[1280,320]{1,0:T(8,128)(2,1)S(1)}, bf16[1280,320]{1,0:T(8,128)(2,1)}, u32[]{:S(2)}) copy-start(bf16[1280,320]{1,0:T(8,128)(2,1)} %copy-done.22) | copy-start | bytes 2457604
  1127.7 23.6 %copy-start.38 = (bf16[512,5,64]{0,2,1:T(8,128)(2,1)S(1)}, bf16[512,5,64]{0,2,1:T(8,128)(2,1)}, u32[]{:S(2)}) copy-start(bf16[512,5,64]{0,2,1:T(8,128)(2,1)} %slice.82) | copy-start | bytes 983044
  1127.7 23.6 %copy-start.47 = (bf16[512,320]{0,1:T(8,128)(2,1)S(1)}, bf16[512,320]{0,1:T(8,128)(2,1)}, u32[]{:S(2)}) copy-start(bf16[512,320]{0,1:T(8,128)(2,1)} %reduce-scatter.35.cloned.1.call-done) | copy-start | bytes 983044
  1151.2 7.3 copy-start.57
  1151.2 7.3 copy-start.58
  1151.2 7.3 copy-start.61
  1151.2 7.3 copy-start.62
  1151.2 134.5 %all-reduce.17.cloned.1.call-start = ((), (), s32[]{:S(2)}) async-start(), calls=%async_computation.24 | async-start | bytes 5242880 | tf_op jit(solution)/shard_map/psum | solution.py:239
  1227.3 58.4 %copy-start.54 = (f32[1280]{0:T(1024)S(1)}, f32[1280]{0:T(1024)}, u32[]{:S(2)}) copy-start(f32[1280]{0:T(1024)} %param.32) | copy-start | bytes 15364
  (42 other events, 101.9 us)
Sparse Core Ops, SparseCore 0:
  154.4 189.7 all-reduce.10
  378.1 187.8 all-reduce.12
  600.6 187.8 all-reduce.14
  1158.6 104.0 all-reduce.16
Sparse Core Ops, SparseCore 1:
  156.3 29.9 all-gather.5
  187.7 29.1 all-gather.3
  218.3 29.1 all-gather.7
  885.4 14.9 reduce-scatter.32
  902.6 16.0 reduce-scatter.34
  921.3 24.3 reduce-scatter.60
  948.1 38.5 reduce-scatter.44
  989.1 38.5 reduce-scatter.36
  1030.1 38.5 reduce-scatter.40
  1071.9 24.3 reduce-scatter.56
  1099.3 24.3 reduce-scatter.52
  1126.8 24.3 reduce-scatter.48
  1153.3 11.8 reduce-scatter.62
  1167.4 18.7 reduce-scatter.46
  1188.4 24.0 reduce-scatter.38
  1214.7 19.7 reduce-scatter.42
  1236.8 13.3 reduce-scatter.58
  1252.4 13.1 reduce-scatter.54
  1267.6 11.5 reduce-scatter.50
where the time goes:
time: 1310 us; the launch traced here: 1300 us
  waiting for transfers between devices  788 us (60%)
  matrix products  205 us (16%)
  blocking collectives  158 us (12%)
  other arithmetic  74.7 us (6%)
  local copies, waits for them, and re-layouts  54.5 us (4%)
  between operations  17.3 us (1%)
    psum x1, waiting for transfers between devices, on_device(): attn_out = lax.psum(attn_terms, 'tensor')  188 us
    psum x1, waiting for transfers between devices, on_device(): grad_after = grad_after + lax.psum(input_terms, 'tensor')  188 us
    psum x1, waiting for transfers between devices, on_device(): merged = lax.psum(merged_terms, 'tensor')  188 us
    unnamed x28, waiting for transfers between devices  77.3 us
    dot_general x17, matrix products, outer_sum(): lax.dot_general(left, right, (((0,), (0,)), ((), ())), preferred_element_...  51.7 us
    reduce_scatter x1, waiting for transfers between devices, on_device(): lax.psum_scatter(grad_gate.astype(jnp.bfloat16), 'shards', scatter_dimens...  40.9 us
    reduce_scatter x1, waiting for transfers between devices, on_device(): lax.psum_scatter(grad_down.astype(jnp.bfloat16), 'shards', scatter_dimens...  40.9 us
    reduce_scatter x1, waiting for transfers between devices, on_device(): lax.psum_scatter(grad_up.astype(jnp.bfloat16), 'shards', scatter_dimensio...  40.9 us
  transfers between devices with their start and end apart: 23, of which 15 were waited for; matrix products, arithmetic and copies ran while one was open for 8% of the time, Pallas kernels for 0%

commit v1 on v0

--- a/solution.py
+++ b/solution.py
@@ -154,7 +154,11 @@
     mixed_heads, log_totals = lax.map(attend_head, (query_heads, key_heads, value_heads))
     mixed_low = from_heads(mixed_heads)
     attn_terms = jnp.dot(mixed_low, full_output, preferred_element_type=jnp.float32)
-    attn_out = lax.psum(attn_terms, "tensor")
+    attn_out = attn_terms
+    for hop in (1, 2):
+        attn_out = attn_out + lax.ppermute(
+            attn_out, "tensor", [(dev, dev ^ hop) for dev in range(4)]
+        )
     after_attn, attn_back = jax.vjp(residual_step, tokens.astype(jnp.float32), attn_out, alpha_attn)
     after_low = after_attn.astype(jnp.bfloat16)
     up_proj = jnp.dot(after_low, full_up, preferred_element_type=jnp.float32)

time: 1310 us -> 1570 us (1.20)
  waiting for transfers between devices: 788 us -> 1040 us
    ppermute x0 -> x2, waiting for transfers between devices: none -> 339 us  [on_device(): lax.ppermute(attn_out, 'tensor', [(dev, dev ^ hop) for dev in range(4)])]
    psum x1 -> x0, waiting for transfers between devices: 188 us -> none  [on_device(): attn_out = lax.psum(attn_terms, 'tensor')]
    psum x1, waiting for transfers between devices: 0.01 us -> 100 us  [on_device(): lax.psum(token_terms.astype(jnp.bfloat16), 'tensor').astype(jnp.float32)]
    unnamed x28 -> x27, waiting for transfers between devices: 77.3 us -> 76.6 us
  transfers between devices with their start and end apart: 23 -> 24, of which waited for: 15 -> 17; matrix products, arithmetic and copies ran while one was open for 8% -> 7% of each run, Pallas kernels for 0% -> 0%
where the time goes in v1:
time: 1570 us; the launch traced here: 1560 us
  waiting for transfers between devices  1040 us (66%)
  matrix products  205 us (13%)
  blocking collectives  156 us (10%)
  other arithmetic  83.4 us (5%)
  local copies, waits for them, and re-layouts  53.4 us (3%)
  between operations  15.9 us (1%)
    ppermute x2, waiting for transfers between devices, on_device(): lax.ppermute(attn_out, 'tensor', [(dev, dev ^ hop) for dev in range(4)])  339 us
    psum x1, waiting for transfers between devices, on_device(): merged = lax.psum(merged_terms, 'tensor')  189 us
    psum x1, waiting for transfers between devices, on_device(): grad_after = grad_after + lax.psum(input_terms, 'tensor')  188 us
    psum x1, waiting for transfers between devices, on_device(): lax.psum(token_terms.astype(jnp.bfloat16), 'tensor').astype(jnp.float32)  100 us
    unnamed x27, waiting for transfers between devices  76.6 us
    dot_general x17, matrix products, outer_sum(): lax.dot_general(left, right, (((0,), (0,)), ((), ())), preferred_element_...  51.7 us
    reduce_scatter x1, waiting for transfers between devices, on_device(): lax.psum_scatter(grad_down.astype(jnp.bfloat16), 'shards', scatter_dimens...  41.2 us
    reduce_scatter x1, waiting for transfers between devices, on_device(): lax.psum_scatter(grad_gate.astype(jnp.bfloat16), 'shards', scatter_dimens...  41.2 us
  transfers between devices with their start and end apart: 24, of which 17 were waited for; matrix products, arithmetic and copies ran while one was open for 7% of the time, Pallas kernels for 0%

profile of v1, /device:TPU:0, one launch (start us, length us, event | category | flops | bytes accessed | tf_op | source)
XLA Modules:
  0.0 1562.1 jit_solution(17469257040741079786)
XLA Ops:
  10.5 11.3 all_gather.48
  21.8 10.1 all_gather.49
  39.1 10.6 all_gather.50
  55.0 9.5 all_gather.51
  65.6 10.8 all_gather.52
  80.7 57.0 %while.28 = (s32[]{:T(128)}, bf16[5,1024,64]{1,2,0:T(8,128)(2,1)S(1)}, f32[5,1024]{1,0:T(8,128)S(1)}, bf16[5,1024,64]{2,1,0:T(8,128)(2,1)}, bf16[5,1536,64]{2,1,...) while((s32[]{:T(128)}, ...), condition=%wide.region_5.6_spmd.clone, body=%wide.region_2.5_spmd.clone.sunk | while | flops 421592064 | bytes 45289628 | solution.py:154
  80.7 3.4 fusion.135
  87.9 4.2 fusion.137
  99.3 4.2 fusion.137
  103.5 3.4 fusion.135
  110.7 4.2 fusion.137
  114.9 3.4 fusion.135
  122.1 4.2 fusion.137
  133.5 4.2 fusion.137
  139.1 9.3 all_gather.53
  148.5 4.0 fusion.72
  154.1 114.0 %collective-permute-done = f32[1024,1280]{1,0:T(8,128)} collective-permute-done((f32[1024,1280]{1,0:T(8,128)}, f32[1024,1280]{1,0:T(8,128)}, u32[]{:S(2)}, u32[]{:S(2)}) %collective-permute-start) | collective-permute-done | bytes 5242912 | tf_op jit(solution)/shard_map/ppermute | solution.py:159
  268.0 7.1 add.187
  278.5 224.6 %collective-permute-done.1 = f32[1024,1280]{1,0:T(8,128)} collective-permute-done((f32[1024,1280]{1,0:T(8,128)}, f32[1024,1280]{1,0:T(8,128)}, u32[]{:S(2)}, u32[]{:S(2)}) %collective-permute-start.1) | collective-permute-done | bytes 5242912 | tf_op jit(solution)/shard_map/ppermute | solution.py:159
  503.1 4.7 multiply_reduce_fusion.11
  512.9 8.1 fusion.73
  521.0 8.7 multiply_convert_fusion.4
  529.7 8.7 fusion.74
  538.9 189.3 %all-reduce.10.cloned.1.call-done = f32[1024,1280]{1,0:T(8,128)} async-done(((f32[1024,1280]{1,0:T(8,128)}), f32[1024,1280]{1,0:T(8,128)}) %all-reduce.10.cloned.1.call-update) | async-done | bytes 5242896 | tf_op jit(solution)/shard_map/psum | solution.py:169
  732.3 4.7 fusion.49
  743.3 9.5 multiply_reduce_fusion.1
  752.9 3.6 fusion.75
  757.2 5.5 convolution_add_fusion
  763.0 187.8 %all-reduce.12.cloned.1.call-done = f32[1024,1280]{1,0:T(8,128)} async-done(((f32[1024,1280]{1,0:T(8,128)}), f32[1024,1280]{1,0:T(8,128)}) %all-reduce.12.cloned.1.call-update) | async-done | bytes 5242896 | tf_op jit(solution)/shard_map/psum | solution.py:183
  950.7 9.5 multiply_reduce_fusion.3
  960.3 11.6 multiply_reduce_fusion.4
  976.7 68.5 %while.29 = (s32[]{:T(128)}, f32[5,1024,64]{1,2,0:T(8,128)}, f32[5,1536,64]{1,2,0:T(8,128)}, bf16[5,1536,64]{1,2,0:T(8,128)(2,1)}, bf16[5,1024,64]{2,1,0:T(8,128...) while((s32[]{:T(128)}, f32[5,1024,64]{1,2,0:T(8,128)}, ...), condition=%wide.region_18.19_spmd.clone, body=%wide.region_16.18_spmd.clone.sunk | while | flops 1027243008 | bytes 50515088 | solution.py:205
  978.7 4.5 multiply_reduce_fusion.18
  992.4 4.5 multiply_reduce_fusion.18
  1006.1 4.5 multiply_reduce_fusion.18
  1019.8 4.5 multiply_reduce_fusion.18
  1033.5 4.5 multiply_reduce_fusion.18
  1050.0 3.8 convolution_convert_fusion.3
  1056.1 6.8 convolution_convert_fusion
  1064.6 6.7 convolution_convert_fusion.2
  1071.4 7.5 convolution_convert_fusion.1
  1083.9 4.0 fusion.57
  1108.2 41.2 %reduce-scatter.45.cloned.1.call-done = bf16[1280,320]{0,1:T(8,128)(2,1)} async-done(((bf16[1280,1280]{0,1:T(8,128)(2,1)}), bf16[1280,320]{0,1:T(8,128)(2,1)}) %reduce-scatter.45.cloned.1.call-update) | async-done | bytes 819216 | tf_op jit(solution)/shard_map/reduce_scatter | solution.py:265
  1149.5 41.1 %reduce-scatter.37.cloned.1.call-done = bf16[320,1280]{1,0:T(8,128)(2,1)} async-done(((bf16[1280,1280]{1,0:T(8,128)(2,1)}), bf16[320,1280]{1,0:T(8,128)(2,1)}) %reduce-scatter.37.cloned.1.call-update) | async-done | bytes 819216 | tf_op jit(solution)/shard_map/reduce_scatter | solution.py:259
  1190.7 41.2 %reduce-scatter.41.cloned.1.call-done = bf16[320,1280]{1,0:T(8,128)(2,1)} async-done(((bf16[1280,1280]{1,0:T(8,128)(2,1)}), bf16[320,1280]{1,0:T(8,128)(2,1)}) %reduce-scatter.41.cloned.1.call-update) | async-done | bytes 819216 | tf_op jit(solution)/shard_map/reduce_scatter | solution.py:262
  1232.0 27.4 %reduce-scatter.57.cloned.1.call-done = bf16[320,320]{1,0:T(8,128)(2,1)} async-done(((bf16[1280,320]{1,0:T(8,128)(2,1)}), bf16[320,320]{1,0:T(8,128)(2,1)}) %reduce-scatter.57.cloned.1.call-update) | async-done | bytes 204816
  1259.4 27.5 %reduce-scatter.53.cloned.1.call-done = bf16[320,320]{1,0:T(8,128)(2,1)} async-done(((bf16[1280,320]{1,0:T(8,128)(2,1)}), bf16[320,320]{1,0:T(8,128)(2,1)}) %reduce-scatter.53.cloned.1.call-update) | async-done | bytes 204816
  1287.0 3.9 fusion.77
  1291.0 3.9 fusion.76
  1294.8 19.5 %reduce-scatter.49.cloned.1.call-done = bf16[320,320]{1,0:T(8,128)(2,1)} async-done(((bf16[1280,320]{1,0:T(8,128)(2,1)}), bf16[320,320]{1,0:T(8,128)(2,1)}) %reduce-scatter.49.cloned.1.call-update) | async-done | bytes 204816
  1314.5 7.1 add_convert_fusion.1
  1321.7 26.1 %all-reduce.5 = (f32[320]{0:T(512)}, f32[1280]{0:T(1024)}, f32[1280]{0:T(1024)}, f32[1280]{0:T(1024)}, f32[1280]{0:T(1024)}) all-reduce(f32[320]{0:T(512)S(1)} %add.202, f32[1280]{0:T(1024)S(1)} %copy-done.58, f32[1280]{0:T(1024)S(1)} %copy-done.57, ...), channel_id=1, replica_groups=mesh['shards'=4,'context'=2,'tensor'=4] {'shards','context'}, use_global_device_ids=true, to_apply=%region_40.41 | all-reduce | flops 5440 | bytes 43520 | tf_op jit(solution)/shard_map/psum | solution.py:315
  1347.8 5.7 all_gather.60
  1354.5 18.9 %all_gather.63 = bf16[1280,320]{0,1:T(8,128)(2,1)S(1)} all-gather(bf16[1280,160]{0,1:T(8,128)(2,1)} %reduce-scatter.47.cloned.1.call-done), channel_id=1, replica_groups=mesh['shards'=4,'context'=2,'tensor'=4] {'context'}, dimensions={1}, use_global_device_ids=true | all-gather | bytes 1228800 | tf_op jit(solution)/shard_map/all_gather | solution.py:311
  1375.0 13.0 all_gather.61
  1389.3 7.8 reduce-scatter.43.cloned.1.call-done
  1397.2 12.9 all_gather.62
  1412.9 6.0 all_gather.59
  1419.7 8.5 reduce-scatter.55.cloned.1.call-done
  1428.3 5.7 all_gather.58
  1434.8 7.3 reduce-scatter.51.cloned.1.call-done
  1442.1 5.8 all_gather.57
  1448.7 100.5 %all-reduce.14.cloned.1.call-done = bf16[1024,1280]{1,0:T(8,128)(2,1)} async-done(((bf16[1024,1280]{1,0:T(8,128)(2,1)}), bf16[1024,1280]{1,0:T(8,128)(2,1)}) %all-reduce.14.cloned.1.call-update) | async-done | bytes 2621456 | tf_op jit(solution)/shard_map/psum | solution.py:243
  1549.1 5.7 add_convert_fusion
  (345 shorter events, 163.7 us)
Async XLA Ops:
  7.2 505.7 %all-gather.6.cloned.1.call-start = ((), (), s32[]{:S(2)}) async-start(), calls=%async_computation.17 | async-start | bytes 4096000 | tf_op jit(solution)/shard_map/all_gather | solution.py:95
  21.8 13.3 copy-start.24
  21.8 13.3 copy-start.15
  37.7 13.1 copy-start.43
  38.6 12.1 copy-start.45
  38.7 12.1 copy-start.55
  50.7 13.7 copy-start.16
  65.6 15.1 copy-start.35
  65.6 15.1 copy-start.59
  65.6 15.1 copy-start.64
  137.7 14.7 copy-start.36
  152.4 115.6 %collective-permute-start = (f32[1024,1280]{1,0:T(8,128)}, f32[1024,1280]{1,0:T(8,128)}, u32[]{:S(2)}, u32[]{:S(2)}) collective-permute-start(f32[1024,1280]{1,0:T(8,128)} %fusion.72), channel_id=1, source_target_pairs={{0,1},{1,0},{2,3},{3,2},{4,5},{5,4},{6,7},{7,6},{8,9},{9,8},{10,11... | collective-permute-start | bytes 15728648 | tf_op jit(solution)/shard_map/ppermute | solution.py:159
  154.0 367.0 %all-gather.4.cloned.1.call-start = ((), (), s32[]{:S(2)}) async-start(), calls=%async_computation.16 | async-start | bytes 4096000 | tf_op jit(solution)/shard_map/all_gather | solution.py:94
  275.1 228.0 %collective-permute-start.1 = (f32[1024,1280]{1,0:T(8,128)}, f32[1024,1280]{1,0:T(8,128)}, u32[]{:S(2)}, u32[]{:S(2)}) collective-permute-start(f32[1024,1280]{1,0:T(8,128)} %add.187), channel_id=1, source_target_pairs={{0,2},{1,3},{2,0},{3,1},{4,6},{5,7},{6,4},{7,5},{8,10},{9,11},{10,... | collective-permute-start | bytes 15728648 | tf_op jit(solution)/shard_map/ppermute | solution.py:159
  277.7 252.0 %all-gather.8.cloned.1.call-start = ((), (), s32[]{:S(2)}) async-start(), calls=%async_computation.18 | async-start | bytes 4096000 | tf_op jit(solution)/shard_map/all_gather | solution.py:96
  278.5 229.4 %copy-start.53 = (f32[1280]{0:T(1024)S(1)}, f32[1280]{0:T(1024)}, u32[]{:S(2)}) copy-start(f32[1280]{0:T(1024)} %param.32) | copy-start | bytes 15364
  278.5 449.8 %all-reduce.10.cloned.1.call-start = ((), (), s32[]{:S(2)}) async-start(), calls=%async_computation.19 | async-start | bytes 10485760 | tf_op jit(solution)/shard_map/psum | solution.py:169
  512.8 8.2 copy-start.30
  512.8 8.2 copy-start.69
  512.8 8.2 copy-start.70
  538.4 192.9 %copy-start.4 = (bf16[1024,1280]{1,0:T(8,128)(2,1)S(1)}, bf16[1024,1280]{1,0:T(8,128)(2,1)}, u32[]{:S(2)}) copy-start(bf16[1024,1280]{1,0:T(8,128)(2,1)} %param.21) | copy-start | bytes 7864324
  538.4 192.9 %copy-start.52 = (f32[1280]{0:T(1024)S(1)}, f32[1280]{0:T(1024)}, u32[]{:S(2)}) copy-start(f32[1280]{0:T(1024)} %param.33) | copy-start | bytes 15364
  538.5 412.3 %all-reduce.12.cloned.1.call-start = ((), (), s32[]{:S(2)}) async-start(), calls=%async_computation.20 | async-start | bytes 10485760 | tf_op jit(solution)/shard_map/psum | solution.py:183
  731.3 5.7 slice-start
  737.0 6.3 slice-start.4
  743.3 9.6 copy-start.32
  743.3 9.6 copy-start.67
  762.7 319.2 %reduce-scatter.33.cloned.1.call-start = ((), (), s32[]{:S(2)}) async-start(), calls=%async_computation.21 | async-start | bytes 983040 | tf_op jit(solution)/shard_map/reduce_scatter | solution.py:211
  950.7 9.5 copy-start.6
  960.3 11.7 slice-start.2
  960.3 11.7 slice-start.3
  1047.6 36.2 %reduce-scatter.35.cloned.1.call-start = ((), (), s32[]{:S(2)}) async-start(), calls=%async_computation.22 | async-start | bytes 983040 | tf_op jit(solution)/shard_map/reduce_scatter | solution.py:217
  1049.7 6.4 copy-start.33
  1049.7 58.4 %reduce-scatter.61.cloned.1.call-start = ((), (), s32[]{:S(2)}) async-start(), calls=%async_computation.36 | async-start | bytes 1228800
  1056.0 93.4 %reduce-scatter.45.cloned.1.call-start = ((), (), s32[]{:S(2)}) async-start(), calls=%async_computation.28 | async-start | bytes 4096000 | tf_op jit(solution)/shard_map/reduce_scatter | solution.py:265
  1062.9 127.7 %reduce-scatter.37.cloned.1.call-start = ((), (), s32[]{:S(2)}) async-start(), calls=%async_computation.24 | async-start | bytes 4096000 | tf_op jit(solution)/shard_map/reduce_scatter | solution.py:259
  1071.4 160.5 %reduce-scatter.41.cloned.1.call-start = ((), (), s32[]{:S(2)}) async-start(), calls=%async_computation.26 | async-start | bytes 4096000 | tf_op jit(solution)/shard_map/reduce_scatter | solution.py:262
  1079.0 180.3 %reduce-scatter.57.cloned.1.call-start = ((), (), s32[]{:S(2)}) async-start(), calls=%async_computation.34 | async-start | bytes 1228800
  1083.8 6.4 copy-start.8
  1083.8 6.4 copy-start.10
  1083.8 6.4 copy-start.12
  1083.8 6.4 copy-start.14
  1083.8 6.4 copy-start.44
  1083.8 6.4 copy-start.46
  1083.8 6.4 copy-start.56
  1090.1 196.8 %reduce-scatter.53.cloned.1.call-start = ((), (), s32[]{:S(2)}) async-start(), calls=%async_computation.32 | async-start | bytes 1228800
  1100.1 214.2 %reduce-scatter.49.cloned.1.call-start = ((), (), s32[]{:S(2)}) async-start(), calls=%async_computation.30 | async-start | bytes 1228800
  1104.6 182.4 %copy-start.27 = (bf16[1280,320]{1,0:T(8,128)(2,1)S(1)}, bf16[1280,320]{1,0:T(8,128)(2,1)}, u32[]{:S(2)}) copy-start(bf16[1280,320]{1,0:T(8,128)(2,1)} %copy-done.26) | copy-start | bytes 2457604
  1106.9 240.9 %reduce-scatter.63.cloned.1.call-start = ((), (), s32[]{:S(2)}) async-start(), calls=%async_computation.37 | async-start | bytes 368640
  1108.2 246.3 %reduce-scatter.47.cloned.1.call-start = ((), (), s32[]{:S(2)}) async-start(), calls=%async_computation.29 | async-start | bytes 1228800 | tf_op jit(solution)/shard_map/reduce_scatter | solution.py:288
  1149.5 225.6 %reduce-scatter.39.cloned.1.call-start = ((), (), s32[]{:S(2)}) async-start(), calls=%async_computation.25 | async-start | bytes 1228800 | tf_op jit(solution)/shard_map/reduce_scatter | solution.py:282
  1190.6 206.6 %reduce-scatter.43.cloned.1.call-start = ((), (), s32[]{:S(2)}) async-start(), calls=%async_computation.27 | async-start | bytes 1228800 | tf_op jit(solution)/shard_map/reduce_scatter | solution.py:285
  1231.9 181.0 %reduce-scatter.59.cloned.1.call-start = ((), (), s32[]{:S(2)}) async-start(), calls=%async_computation.35 | async-start | bytes 368640 | tf_op jit(solution)/shard_map/reduce_scatter | solution.py:276
  1259.4 168.9 %reduce-scatter.55.cloned.1.call-start = ((), (), s32[]{:S(2)}) async-start(), calls=%async_computation.33 | async-start | bytes 368640 | tf_op jit(solution)/shard_map/reduce_scatter | solution.py:273
  1287.0 155.1 %reduce-scatter.51.cloned.1.call-start = ((), (), s32[]{:S(2)}) async-start(), calls=%async_computation.31 | async-start | bytes 368640 | tf_op jit(solution)/shard_map/reduce_scatter | solution.py:270
  1291.0 23.5 %copy-start.23 = (bf16[1280,320]{1,0:T(8,128)(2,1)S(1)}, bf16[1280,320]{1,0:T(8,128)(2,1)}, u32[]{:S(2)}) copy-start(bf16[1280,320]{1,0:T(8,128)(2,1)} %copy-done.22) | copy-start | bytes 2457604
  1291.0 23.5 %copy-start.38 = (bf16[512,5,64]{0,2,1:T(8,128)(2,1)S(1)}, bf16[512,5,64]{0,2,1:T(8,128)(2,1)}, u32[]{:S(2)}) copy-start(bf16[512,5,64]{0,2,1:T(8,128)(2,1)} %slice.82) | copy-start | bytes 983044
  1291.0 23.5 %copy-start.47 = (bf16[512,320]{0,1:T(8,128)(2,1)S(1)}, bf16[512,320]{0,1:T(8,128)(2,1)}, u32[]{:S(2)}) copy-start(bf16[512,320]{0,1:T(8,128)(2,1)} %reduce-scatter.35.cloned.1.call-done) | copy-start | bytes 983044
  1314.4 7.3 copy-start.57
  1314.4 7.3 copy-start.58
  1314.4 7.3 copy-start.61
  1314.4 7.3 copy-start.62
  1314.4 234.7 %all-reduce.14.cloned.1.call-start = ((), (), s32[]{:S(2)}) async-start(), calls=%async_computation.23 | async-start | bytes 5242880 | tf_op jit(solution)/shard_map/psum | solution.py:243
  1389.3 159.8 %copy-start.54 = (f32[1280]{0:T(1024)S(1)}, f32[1280]{0:T(1024)}, u32[]{:S(2)}) copy-start(f32[1280]{0:T(1024)} %param.32) | copy-start | bytes 15364
  (43 other events, 107.8 us)
Sparse Core Ops, SparseCore 0:
  154.1 29.0 all-gather.5
  277.8 28.0 all-gather.3
  307.5 29.2 all-gather.7
  538.6 189.6 all-reduce.9
  762.9 187.8 all-reduce.11
  1047.7 15.0 reduce-scatter.32
  1065.0 16.0 reduce-scatter.34
  1083.7 24.3 reduce-scatter.60
  1110.7 38.6 reduce-scatter.44
  1151.9 38.6 reduce-scatter.36
  1193.2 38.6 reduce-scatter.40
  1234.9 24.3 reduce-scatter.56
  1262.5 24.3 reduce-scatter.52
  1289.9 24.3 reduce-scatter.48
  1316.4 11.9 reduce-scatter.62
  1330.5 18.7 reduce-scatter.46
  1351.4 23.6 reduce-scatter.38
  1377.1 19.9 reduce-scatter.42
  1399.4 13.4 reduce-scatter.58
  1415.0 13.1 reduce-scatter.54
  1430.5 11.5 reduce-scatter.50
  1445.0 104.0 all-reduce.13
